TPU v7x, 512 devices: a whole 4x8x8 slice. The times are simulated.
512 devices in a mesh: dp: 64 (over z_hi, y, x), blk: 8 (over z_lo, core).
Axes of the slice: x: 4, y: 8, z: 8 (z_hi: 2, z_lo: 4; z = z_hi * 4 + z_lo), core: 2. Of those that a mesh axis runs over, the one named last changes fastest.
Arguments:
- train_act: bfloat16 [2048, 4096], P(('dp', 'blk')), may hold values from -3 to 3
- train_grad: bfloat16 [2048, 8192], P(('dp', 'blk')), may hold values from -3 to 3
- query_act: bfloat16 [256, 4096], P('dp', 'blk'), may hold values from -3 to 3
- query_grad: bfloat16 [256, 8192], P('dp'), may hold values from -3 to 3
- act_basis: bfloat16 [4096, 512], P('blk'), may hold values from -0.25 to 0.25
- grad_basis: bfloat16 [512, 8192], P(None, 'dp'), may hold values from -0.25 to 0.25
- eigenvalues: float32 [4096, 8192], P('blk', 'dp'), may hold values from 0.05 to 5
- example_ids: int32 [2048], replicated, may hold values from 0 to 127, never falling along the last dimension, each value on 1 to 48 neighbouring positions
- query_ids: int32 [256], replicated, may hold values from 0 to 15, never falling along the last dimension, each value on 1 to 48 neighbouring positions
Outputs:
- influence: float32 [128, 16], P('dp')
Inputs may be any that keep to these rules, and one draw needn't show every extreme that they name: `example_ids`: the tokens of one training example are contiguous and ids never fall; every example has a token. `query_ids`: the tokens of one query are contiguous and ids never fall; every query has a token.
All inputs are finite; a program needn't handle non-finite values.
Results may differ from a plain program's by a relative error of at most 0.0007.
The roundings to bfloat16 on the way count: a program that leaves them out, or rounds other values in their place, can miss the bound.
Values may be sent and summed in bfloat16 or wider, within the bound.
No kernel may reach another device: no remote copies, remote signals or barrier semaphores. Data moves between devices by JAX's collectives and lax.ppermute only.
A program may use at most 64 MiB of HBM per device.

v0:
```python
import jax
import jax.numpy as jnp
from jax import lax
from jax.sharding import PartitionSpec as P

D = 4096
FF = 8192
QUERIES = 16
EX_DP = 2


def partner(block, axis, stride):
    count = lax.axis_size(axis)
    route = []
    for low in range(count):
        high = low | 1 << stride
        if high != low and high < count:
            route += [(low, high), (high, low)]
    return lax.ppermute(block, axis, route)


def rotate_blocks(row_data, basis):
    row_count = row_data.shape[0]
    block_size = basis.shape[1]
    count_blocks = basis.shape[0] // block_size
    turned = jnp.einsum(
        "tnk,nkl->tnl",
        row_data.reshape(row_count, count_blocks, block_size),
        basis.reshape(count_blocks, block_size, block_size),
        preferred_element_type=jnp.float32,
    )
    return turned.reshape(row_count, count_blocks * block_size).astype(jnp.bfloat16)


def rotate_columns(row_data, basis):
    row_count = row_data.shape[0]
    full_width = row_data.shape[1]
    block_size = basis.shape[0]
    col_width = basis.shape[1]
    count_blocks = full_width // block_size
    turned = jnp.einsum(
        "tmk,kml->tml",
        row_data.reshape(row_count, count_blocks, block_size),
        basis.reshape(block_size, count_blocks, col_width // count_blocks),
        preferred_element_type=jnp.float32,
    )
    return turned.reshape(row_count, col_width).astype(jnp.bfloat16)


def join_pair(mine, other, is_upper):
    return jnp.where(is_upper, jnp.concatenate([other, mine], 1), jnp.concatenate([mine, other], 1))


def shards(
    train_act,
    train_grad,
    query_act,
    query_grad,
    act_basis,
    grad_basis,
    eigenvalues,
    example_ids,
    query_ids,
):
    devices_dp = lax.axis_size("dp")
    block_size = grad_basis.shape[0]
    col_width = grad_basis.shape[1]
    owned_width = act_basis.shape[0]
    eigen_sum = lax.psum(jnp.sum(eigenvalues), ("dp", "blk"))
    damping = 0.1 * eigen_sum / (D * FF)
    owned_rows = lax.all_to_all(train_act, "blk", split_axis=1, concat_axis=0, tiled=True)
    query_all = lax.all_gather(rotate_blocks(query_act, act_basis), "dp", axis=0, tiled=True)
    train_cols, query_cols = (
        lax.all_to_all(train_grad, "dp", split_axis=1, concat_axis=0, tiled=True),
        lax.all_to_all(query_grad, "dp", split_axis=1, concat_axis=0, tiled=True),
    )
    position = lax.axis_index("dp")
    for bit_index in range((block_size // col_width).bit_length() - 1):
        other_train, other_query = partner((train_cols, query_cols), "dp", bit_index)
        is_upper = position >> bit_index & 1 == 1
        train_cols = join_pair(train_cols, other_train, is_upper)
        query_cols = join_pair(query_cols, other_query, is_upper)
    grad_mine = rotate_columns(train_cols, grad_basis)
    query_grad_rot = rotate_columns(query_cols, grad_basis)
    grad_all = lax.all_gather(
        grad_mine.reshape(devices_dp, 1, grad_mine.shape[0] // devices_dp, col_width),
        "blk",
        axis=1,
        tiled=True,
    )
    grad_all = grad_all.reshape(
        grad_all.shape[0] * grad_all.shape[1] * grad_all.shape[2], col_width
    )
    one_query = (query_ids[:, None] == jnp.arange(QUERIES, dtype=jnp.int32)[None, :]).astype(
        jnp.bfloat16
    )
    weighted = one_query.T[:, :, None] * query_all[None, :, :]
    query_gram = jnp.einsum(
        "qti,tj->iqj", weighted, query_grad_rot, preferred_element_type=jnp.float32
    )
    norm_scale = float(D * FF) ** (-0.5)
    precond = (query_gram / (eigenvalues[:, None, :] + damping) * norm_scale).astype(jnp.bfloat16)
    precond = precond.reshape(owned_width, QUERIES * col_width)
    shard_rows = lax.all_gather(rotate_blocks(owned_rows, act_basis), "dp", axis=0, tiled=True)
    row_count = shard_rows.shape[0]
    mixed_rows = jnp.dot(shard_rows, precond, preferred_element_type=jnp.float32).reshape(
        row_count, QUERIES, col_width
    )
    token_score = jnp.sum(mixed_rows * grad_all[:, None, :].astype(jnp.float32), axis=2)
    example_count = EX_DP * devices_dp
    one_example = (
        example_ids[:, None] == jnp.arange(example_count, dtype=jnp.int32)[None, :]
    ).astype(jnp.float32)
    partial_scores = jnp.dot(one_example.T, token_score, precision=lax.Precision.HIGHEST)
    all_scores = lax.psum(partial_scores, ("dp", "blk"))
    return lax.dynamic_slice_in_dim(all_scores, lax.axis_index("dp") * EX_DP, EX_DP, 0)


def solution(mesh):
    placed = (
        P(("dp", "blk"), None),
        P(("dp", "blk"), None),
        P("dp", "blk"),
        P("dp", None),
        P("blk", None),
        P(None, "dp"),
        P("blk", "dp"),
        P(),
        P(),
    )
    return jax.shard_map(
        shards, mesh=mesh, in_specs=placed, out_specs=P("dp", None), check_vma=False
    )
```

profile of v0, /device:TPU:1, one launch (start us, length us, event | category | flops | bytes accessed | tf_op | source)
XLA Modules:
  0.0 528.6 jit_solution(4616958831097814002)
XLA Ops:
  6.5 0.0 copy-start
  6.5 15.2 %all_to_all.54 = bf16[4,8,512]{2,0,1:T(4,128)(2,1)S(1)} all-to-all(bf16[4,8,512]{2,0,1:T(4,128)(2,1)} %bitcast.73), channel_id=1, replica_groups=mesh['dp'=64,'blk'=8] {'blk'}, dimensions={1} | all-to-all | bytes 65536 | tf_op jit(solution)/shard_map/all_to_all | solution.py:71
  21.8 0.0 copy-done
  21.8 0.8 fusion.10
  22.6 0.0 all-gather.4.cloned.1.call-update
  22.6 1.6 reduce_sum.18
  24.2 14.7 %all-to-all-start.2 = ((bf16[4,64,128]{2,0,1:T(4,128)(2,1)}), bf16[4,64,128]{2,0,1:T(4,128)(2,1)S(1)}, u32[]{:S(2)}, u32[]{:S(2)}) async-start(bf16[4,64,128]{2,0,1:T(4,128)(2,1)} %bitcast.71), calls=%async_computation.2 | async-start | bytes 131072 | tf_op jit(solution)/shard_map/all_to_all | solution.py:74
  38.9 104.2 %psum.14 = f32[]{:T(128)} all-reduce(f32[]{:T(128)} %reduce_sum.18), channel_id=1, replica_groups=mesh['dp'=64,'blk'=8] {'dp','blk'}, use_global_device_ids=true, to_apply=%region_1.0 | all-reduce | flops 1 | bytes 8 | tf_op jit(solution)/shard_map/psum | solution.py:69
  143.7 1.0 broadcast_add_fusion
  144.7 0.7 fusion.34
  145.4 0.0 all-to-all-done.2
  145.4 10.7 %all-to-all-start.1 = ((bf16[4,64,128]{2,0,1:T(4,128)(2,1)}), bf16[4,64,128]{2,0,1:T(4,128)(2,1)S(1)}, u32[]{:S(2)}, u32[]{:S(2)}) async-start(bf16[4,64,128]{2,0,1:T(4,128)(2,1)} %bitcast.72), calls=%async_computation.1 | async-start | bytes 131072 | tf_op jit(solution)/shard_map/all_to_all | solution.py:75
  156.1 2.9 collective-permute-start.2
  159.0 0.9 fusion.11
  159.9 9.7 %all-to-all-done.1 = bf16[4,64,128]{2,0,1:T(4,128)(2,1)S(1)} async-done(((bf16[4,64,128]{2,0,1:T(4,128)(2,1)}), bf16[4,64,128]{2,0,1:T(4,128)(2,1)S(1)}, u32[]{:S(2)}, u32[]{:S(2)}) %all-to-all-start.1) | async-done | bytes 65568 | tf_op jit(solution)/shard_map/all_to_all | solution.py:75
  169.6 2.2 collective-permute-start
  171.8 0.0 collective-permute-done.2
  171.9 3.9 collective-permute-start.3
  175.9 189.5 %all-gather.1 = bf16[256,1,512]{2,1,0:T(2,128)(2,1)S(1)} all-gather(bf16[4,1,512]{2,1,0:T(2,128)(2,1)S(1)} %copy.34), channel_id=3, replica_groups=mesh['dp'=64,'blk'=8] {'dp'}, dimensions={0}, use_global_device_ids=true | all-gather | bytes 266240 | tf_op jit(solution)/shard_map/all_gather | solution.py:72
  365.3 0.1 copy.36
  365.5 0.0 collective-permute-done
  365.5 1.9 collective-permute-start.1
  367.5 0.0 collective-permute-done.3
  367.5 0.2 convolution_convert_fusion
  367.7 45.3 %all_gather.11 = bf16[64,8,4,128]{3,2,1,0:T(4,128)(2,1)S(1)} all-gather(bf16[64,1,4,128]{3,2,1,0:T(4,128)(2,1)S(1)} %bitcast.70), channel_id=1, replica_groups=mesh['dp'=64,'blk'=8] {'blk'}, dimensions={1}, use_global_device_ids=true | all-gather | bytes 589824 | tf_op jit(solution)/shard_map/all_gather | solution.py:85
  413.0 0.2 copy.39
  413.3 0.0 collective-permute-done.1
  413.3 3.0 fusion.2
  416.2 7.7 %multiply_reduce_fusion = f32[2048,16]{0,1:T(8,128)S(1)} fusion(f32[2048,128]{0,1:T(8,128)S(1)} %copy.39, bf16[2048,1,512]{2,0,1:T(8,128)(2,1)} %all-gather.4.cloned.1.call-done, f32[128,16,512]{2,0,1:T(8,128)} %fusion.2, f32[512,128]{0,1:T(8,128)S(1)} %copy.36), kind=kOutput, calls=%fused_computation | convolution fusion | flops 4306468864 | bytes 7733248 | tf_op jit(solution)/shard_map/dot_general | solution.py:106
  424.0 1.1 fusion.13
  425.1 96.1 %psum.15 = f32[128,16]{1,0:T(8,128)S(1)} all-reduce(f32[128,16]{1,0:T(8,128)S(1)} %fusion.13), channel_id=1, replica_groups=mesh['dp'=64,'blk'=8] {'dp','blk'}, use_global_device_ids=true, to_apply=%region_3.4 | all-reduce | flops 2048 | bytes 16384 | tf_op jit(solution)/shard_map/psum | solution.py:115
  521.1 0.6 constant_dynamic-slice_fusion
  (11 shorter events, 0.2 us)
Async XLA Ops:
  6.5 15.2 %copy-start = (bf16[512,512]{1,0:T(8,128)(2,1)S(1)}, bf16[512,512]{1,0:T(8,128)(2,1)}, u32[]{:S(2)}) copy-start(bf16[512,512]{1,0:T(8,128)(2,1)} %param.13) | copy-start | bytes 1572868
  6.5 360.9 %copy-start.1 = (bf16[512,128]{1,0:T(8,128)(2,1)S(1)}, bf16[512,128]{1,0:T(8,128)(2,1)}, u32[]{:S(2)}) copy-start(bf16[512,128]{1,0:T(8,128)(2,1)} %param.14) | copy-start | bytes 393220
  6.5 409.7 %all-gather.4.cloned.1.call-start = ((), (), s32[]{:S(2)}) async-start(), calls=%async_computation.3 | async-start | bytes 2129920 | tf_op jit(solution)/shard_map/all_gather | solution.py:104
  24.2 121.2 %all-to-all-start.2 = ((bf16[4,64,128]{2,0,1:T(4,128)(2,1)}), bf16[4,64,128]{2,0,1:T(4,128)(2,1)S(1)}, u32[]{:S(2)}, u32[]{:S(2)}) async-start(bf16[4,64,128]{2,0,1:T(4,128)(2,1)} %bitcast.71), calls=%async_computation.2 | async-start | bytes 131072 | tf_op jit(solution)/shard_map/all_to_all | solution.py:74
  145.4 24.2 %all-to-all-start.1 = ((bf16[4,64,128]{2,0,1:T(4,128)(2,1)}), bf16[4,64,128]{2,0,1:T(4,128)(2,1)S(1)}, u32[]{:S(2)}, u32[]{:S(2)}) async-start(bf16[4,64,128]{2,0,1:T(4,128)(2,1)} %bitcast.72), calls=%async_computation.1 | async-start | bytes 131072 | tf_op jit(solution)/shard_map/all_to_all | solution.py:75
  156.1 15.7 %collective-permute-start.2 = (bf16[256,128]{1,0:T(8,128)(2,1)S(1)}, bf16[256,128]{1,0:T(8,128)(2,1)S(1)}, u32[]{:S(2)}, u32[]{:S(2)}) collective-permute-start(bf16[256,128]{1,0:T(8,128)(2,1)S(1)} %bitcast.67), channel_id=1, source_target_pairs={{0,8},{8,0},{16,24},{24,16},{32,40},{40,32},{48,56},{56,48},{64,72... | collective-permute-start | bytes 196616 | tf_op jit(solution)/shard_map/ppermute | solution.py:19
  169.6 195.8 %collective-permute-start = (bf16[256,128]{1,0:T(8,128)(2,1)S(1)}, bf16[256,128]{1,0:T(8,128)(2,1)S(1)}, u32[]{:S(2)}, u32[]{:S(2)}) collective-permute-start(bf16[256,128]{1,0:T(8,128)(2,1)S(1)} %bitcast.65), channel_id=1, source_target_pairs={{0,8},{8,0},{16,24},{24,16},{32,40},{40,32},{48,56},{56,48},{64,72... | collective-permute-start | bytes 196616 | tf_op jit(solution)/shard_map/ppermute | solution.py:19
  171.9 195.6 %collective-permute-start.3 = (bf16[256,256]{1,0:T(8,128)(2,1)S(1)}, bf16[256,256]{1,0:T(8,128)(2,1)S(1)}, u32[]{:S(2)}, u32[]{:S(2)}) collective-permute-start(bf16[256,256]{1,0:T(8,128)(2,1)S(1)} %maximum_select_fusion.6), channel_id=1, source_target_pairs={{0,16},{16,0},{8,24},{24,8},{32,48},{48,32},{40,56},{56,40},{64,80... | collective-permute-start | bytes 393224 | tf_op jit(solution)/shard_map/ppermute | solution.py:19
  365.5 47.7 %collective-permute-start.1 = (bf16[256,256]{1,0:T(8,128)(2,1)S(1)}, bf16[256,256]{1,0:T(8,128)(2,1)S(1)}, u32[]{:S(2)}, u32[]{:S(2)}) collective-permute-start(bf16[256,256]{1,0:T(8,128)(2,1)S(1)} %maximum_select_fusion.5), channel_id=1, source_target_pairs={{0,16},{16,0},{8,24},{24,8},{32,48},{48,32},{40,56},{56,40},{64,80... | collective-permute-start | bytes 393224 | tf_op jit(solution)/shard_map/ppermute | solution.py:19
  416.2 7.7 %copy-start.2 = (s32[2048]{0:T(1024)S(1)}, s32[2048]{0:T(1024)}, u32[]{:S(2)}) copy-start(s32[2048]{0:T(1024)} %param.16) | copy-start | bytes 24580
Sparse Core Ops, SparseCore 0:
  22.7 136.6 all-gather.3
where the time goes:
time: 529 us
  blocking collectives  450 us (85%)
  starting transfers between devices  36.4 us (7%)
  between operations  14.2 us (3%)
  matrix products  13.6 us (3%)
  waiting for transfers between devices  9.75 us (2%)
    all_gather x1, blocking collectives, shards(): lax.all_gather(rotate_blocks(query_act, act_basis), 'dp', axis=0, tiled=T...  189 us
    psum x1, blocking collectives, shards(): eigen_sum = lax.psum(jnp.sum(eigenvalues), ('dp', 'blk'))  104 us
    psum x1, blocking collectives, shards(): all_scores = lax.psum(partial_scores, ('dp', 'blk'))  96.1 us
    all_gather x1, blocking collectives, shards(): lax.all_gather(grad_mine.reshape(devices_dp, 1, grad_mine.shape[0] // dev...  45.3 us
    all_to_all x1, blocking collectives, shards(): lax.all_to_all(train_act, 'blk', split_axis=1, concat_axis=0, tiled=True)  15.2 us
    all_to_all x1, starting transfers between devices, shards(): lax.all_to_all(train_grad, 'dp', split_axis=1, concat_axis=0, tiled=True)  14.7 us
    ppermute x4, starting transfers between devices, partner(): return lax.ppermute(block, axis, route)  11 us
    all_to_all x1, starting transfers between devices, shards(): lax.all_to_all(query_grad, 'dp', split_axis=1, concat_axis=0, tiled=True)  10.7 us
  transfers between devices with their start and end apart: 7, of which 1 were waited for; matrix products, arithmetic and copies ran while one was open for 1% of the time, Pallas kernels for 0%

commit v1 on v0

--- a/solution.py
+++ b/solution.py
@@ -112,7 +112,7 @@
         example_ids[:, None] == jnp.arange(example_count, dtype=jnp.int32)[None, :]
     ).astype(jnp.float32)
     partial_scores = jnp.dot(one_example.T, token_score, precision=lax.Precision.HIGHEST)
-    all_scores = lax.psum(partial_scores, ("dp", "blk"))
+    all_scores = jnp.sum(lax.all_gather(partial_scores, ("dp", "blk")), axis=0)
     return lax.dynamic_slice_in_dim(all_scores, lax.axis_index("dp") * EX_DP, EX_DP, 0)
 
 

time: 529 us -> 1200 us (2.27)
  waiting for transfers between devices: 9.75 us -> 777 us
  blocking collectives: 450 us -> 354 us
    all_gather x0 -> x1, waiting for transfers between devices: none -> 767 us  [shards(): all_scores = jnp.sum(lax.all_gather(partial_scores, ('dp', 'blk')), axis=0)]
    psum x1 -> x0, blocking collectives: 96.1 us -> none  [shards(): all_scores = lax.psum(partial_scores, ('dp', 'blk'))]
  transfers between devices with their start and end apart: 7 -> 8, of which waited for: 1 -> 2; matrix products, arithmetic and copies ran while one was open for 1% -> 1% of each run, Pallas kernels for 0% -> 0%
where the time goes in v1:
time: 1200 us
  waiting for transfers between devices  777 us (65%)
  blocking collectives  354 us (30%)
  starting transfers between devices  36.4 us (3%)
  between operations  14.2 us (1%)
  matrix products  13.5 us (1%)
    all_gather x1, waiting for transfers between devices, shards(): all_scores = jnp.sum(lax.all_gather(partial_scores, ('dp', 'blk')), axis=0)  767 us
    all_gather x1, blocking collectives, shards(): lax.all_gather(rotate_blocks(query_act, act_basis), 'dp', axis=0, tiled=T...  189 us
    psum x1, blocking collectives, shards(): eigen_sum = lax.psum(jnp.sum(eigenvalues), ('dp', 'blk'))  104 us
    all_gather x1, blocking collectives, shards(): lax.all_gather(grad_mine.reshape(devices_dp, 1, grad_mine.shape[0] // dev...  45.8 us
  transfers between devices with their start and end apart: 8, of which 2 were waited for; matrix products, arithmetic and copies ran while one was open for 1% of the time, Pallas kernels for 0%

profile of v1, /device:TPU:1, one launch (start us, length us, event | category | flops | bytes accessed | tf_op | source)
XLA Modules:
  0.0 1203.1 jit_solution(15559847975174981257)
XLA Ops:
  6.5 15.2 %all_to_all.54 = bf16[4,8,512]{2,0,1:T(4,128)(2,1)S(1)} all-to-all(bf16[4,8,512]{2,0,1:T(4,128)(2,1)} %bitcast.79), channel_id=1, replica_groups=mesh['dp'=64,'blk'=8] {'blk'}, dimensions={1} | all-to-all | bytes 65536 | tf_op jit(solution)/shard_map/all_to_all | solution.py:71
  21.8 0.8 fusion.10
  22.6 0.0 all-gather.6.cloned.1.call-update
  22.6 1.6 reduce_sum.27
  24.2 14.7 %all-to-all-start.2 = ((bf16[4,64,128]{2,0,1:T(4,128)(2,1)}), bf16[4,64,128]{2,0,1:T(4,128)(2,1)S(1)}, u32[]{:S(2)}, u32[]{:S(2)}) async-start(bf16[4,64,128]{2,0,1:T(4,128)(2,1)} %bitcast.77), calls=%async_computation.2 | async-start | bytes 131072 | tf_op jit(solution)/shard_map/all_to_all | solution.py:74
  38.9 104.2 %psum.7 = f32[]{:T(128)} all-reduce(f32[]{:T(128)} %reduce_sum.27), channel_id=1, replica_groups=mesh['dp'=64,'blk'=8] {'dp','blk'}, use_global_device_ids=true, to_apply=%region_1.0 | all-reduce | flops 1 | bytes 8 | tf_op jit(solution)/shard_map/psum | solution.py:69
  143.7 1.0 broadcast_add_fusion
  144.7 0.7 fusion.32
  145.4 10.6 all-to-all-start.1
  156.1 0.0 all-gather.8.cloned.1.call-start
  156.1 2.9 collective-permute-start.2
  159.0 0.9 fusion.11
  159.9 9.7 all-to-all-done.1
  169.6 2.2 collective-permute-start
  171.8 0.0 collective-permute-done.2
  171.8 4.0 collective-permute-start.3
  175.8 189.0 %all-gather.1 = bf16[256,1,512]{2,1,0:T(2,128)(2,1)S(1)} all-gather(bf16[4,1,512]{2,1,0:T(2,128)(2,1)S(1)} %copy.36), channel_id=3, replica_groups=mesh['dp'=64,'blk'=8] {'dp'}, dimensions={0}, use_global_device_ids=true | all-gather | bytes 266240 | tf_op jit(solution)/shard_map/all_gather | solution.py:72
  364.8 0.1 copy.38
  365.0 1.9 collective-permute-start.1
  367.0 0.2 convolution_convert_fusion
  367.2 45.8 %all_gather.17 = bf16[64,8,4,128]{3,2,1,0:T(4,128)(2,1)S(1)} all-gather(bf16[64,1,4,128]{3,2,1,0:T(4,128)(2,1)S(1)} %bitcast.76), channel_id=1, replica_groups=mesh['dp'=64,'blk'=8] {'blk'}, dimensions={1}, use_global_device_ids=true | all-gather | bytes 589824 | tf_op jit(solution)/shard_map/all_gather | solution.py:85
  413.0 0.2 copy.41
  413.2 0.0 collective-permute-done.1
  413.3 3.0 fusion.2
  416.2 7.5 multiply_reduce_fusion
  423.7 1.2 fusion.12
  424.9 0.0 all-gather.8.cloned.1.call-update
  425.0 767.3 %all-gather.8.cloned.1.call-done = f32[65536,16]{0,1:T(8,128)} async-done(((f32[128,16]{0,1:T(8,128)}), f32[65536,16]{0,1:T(8,128)}) %all-gather.8.cloned.1.call-update) | async-done | bytes 4194320 | tf_op jit(solution)/shard_map/all_gather | solution.py:115
  1192.3 3.0 copy.46
  1195.3 0.2 bitcast_reduce_fusion
  1195.5 0.1 constant_dynamic-slice_fusion
  1195.6 0.6 copy.42
  (16 shorter events, 0.2 us)
Async XLA Ops:
  6.5 15.2 %copy-start = (bf16[512,512]{1,0:T(8,128)(2,1)S(1)}, bf16[512,512]{1,0:T(8,128)(2,1)}, u32[]{:S(2)}) copy-start(bf16[512,512]{1,0:T(8,128)(2,1)} %param.13) | copy-start | bytes 1572868
  6.5 360.4 %copy-start.1 = (bf16[512,128]{1,0:T(8,128)(2,1)S(1)}, bf16[512,128]{1,0:T(8,128)(2,1)}, u32[]{:S(2)}) copy-start(bf16[512,128]{1,0:T(8,128)(2,1)} %param.14) | copy-start | bytes 393220
  6.5 409.7 %all-gather.6.cloned.1.call-start = ((), (), s32[]{:S(2)}) async-start(), calls=%async_computation.3 | async-start | bytes 2129920 | tf_op jit(solution)/shard_map/all_gather | solution.py:104
  24.2 121.2 %all-to-all-start.2 = ((bf16[4,64,128]{2,0,1:T(4,128)(2,1)}), bf16[4,64,128]{2,0,1:T(4,128)(2,1)S(1)}, u32[]{:S(2)}, u32[]{:S(2)}) async-start(bf16[4,64,128]{2,0,1:T(4,128)(2,1)} %bitcast.77), calls=%async_computation.2 | async-start | bytes 131072 | tf_op jit(solution)/shard_map/all_to_all | solution.py:74
  145.4 24.2 %all-to-all-start.1 = ((bf16[4,64,128]{2,0,1:T(4,128)(2,1)}), bf16[4,64,128]{2,0,1:T(4,128)(2,1)S(1)}, u32[]{:S(2)}, u32[]{:S(2)}) async-start(bf16[4,64,128]{2,0,1:T(4,128)(2,1)} %bitcast.78), calls=%async_computation.1 | async-start | bytes 131072 | tf_op jit(solution)/shard_map/all_to_all | solution.py:75
  156.1 1036.2 %all-gather.8.cloned.1.call-start = ((), (), s32[]{:S(2)}) async-start(), calls=%async_computation.4 | async-start | bytes 4202496 | tf_op jit(solution)/shard_map/all_gather | solution.py:115
  156.1 15.7 %collective-permute-start.2 = (bf16[256,128]{1,0:T(8,128)(2,1)S(1)}, bf16[256,128]{1,0:T(8,128)(2,1)S(1)}, u32[]{:S(2)}, u32[]{:S(2)}) collective-permute-start(bf16[256,128]{1,0:T(8,128)(2,1)S(1)} %bitcast.73), channel_id=1, source_target_pairs={{0,8},{8,0},{16,24},{24,16},{32,40},{40,32},{48,56},{56,48},{64,72... | collective-permute-start | bytes 196616 | tf_op jit(solution)/shard_map/ppermute | solution.py:19
  169.6 195.4 %collective-permute-start = (bf16[256,128]{1,0:T(8,128)(2,1)S(1)}, bf16[256,128]{1,0:T(8,128)(2,1)S(1)}, u32[]{:S(2)}, u32[]{:S(2)}) collective-permute-start(bf16[256,128]{1,0:T(8,128)(2,1)S(1)} %bitcast.71), channel_id=1, source_target_pairs={{0,8},{8,0},{16,24},{24,16},{32,40},{40,32},{48,56},{56,48},{64,72... | collective-permute-start | bytes 196616 | tf_op jit(solution)/shard_map/ppermute | solution.py:19
  171.8 195.1 %collective-permute-start.3 = (bf16[256,256]{1,0:T(8,128)(2,1)S(1)}, bf16[256,256]{1,0:T(8,128)(2,1)S(1)}, u32[]{:S(2)}, u32[]{:S(2)}) collective-permute-start(bf16[256,256]{1,0:T(8,128)(2,1)S(1)} %maximum_select_fusion.6), channel_id=1, source_target_pairs={{0,16},{16,0},{8,24},{24,8},{32,48},{48,32},{40,56},{56,40},{64,80... | collective-permute-start | bytes 393224 | tf_op jit(solution)/shard_map/ppermute | solution.py:19
  365.0 48.2 %collective-permute-start.1 = (bf16[256,256]{1,0:T(8,128)(2,1)S(1)}, bf16[256,256]{1,0:T(8,128)(2,1)S(1)}, u32[]{:S(2)}, u32[]{:S(2)}) collective-permute-start(bf16[256,256]{1,0:T(8,128)(2,1)S(1)} %maximum_select_fusion.5), channel_id=1, source_target_pairs={{0,16},{16,0},{8,24},{24,8},{32,48},{48,32},{40,56},{56,40},{64,80... | collective-permute-start | bytes 393224 | tf_op jit(solution)/shard_map/ppermute | solution.py:19
  416.2 7.5 copy-start.2
Sparse Core Ops, SparseCore 0:
  22.7 136.6 all-gather.5
  425.1 767.1 all-gather.7
